TPU v7x, 128 devices: a whole 4x4x4 slice. The times are simulated.
128 devices in a mesh: tm: 32 (over z, y, core), rows: 4 (over x).
Axes of the slice: x: 4, y: 4, z: 4, core: 2. Of those that a mesh axis runs over, the one named last changes fastest.
Arguments:
- covars: bfloat16 [524288, 128], P(('tm', 'rows')), may hold values from -5 to 5
- strata: int32 [524288], P(('tm', 'rows')), may hold values from 0 to 511
- centers: int32 [524288], P(('tm', 'rows')), may hold values from 0 to 2047
- events: int32 [524288], P(('tm', 'rows')), may hold values 0 or 1
- counts: int32 [128], P(('tm', 'rows')), may hold values from 1024 to 4096, as said below
- beta: float32 [128], replicated, may hold values from -0.4 to 0.4
- frailty: float32 [2048], replicated, may hold values from -3 to 3
Outputs:
- score: float32 [128], replicated
- info: float32 [128, 128], replicated
- center_score: float32 [2048], P(('tm', 'rows'))
- center_info: float32 [2048], P(('tm', 'rows'))
- center_cross: float32 [2048, 128], P(('tm', 'rows'))
Inputs may be any that keep to these rules, and one draw needn't show every extreme that they name: `counts`: each shard's live records come first; some shard is full.
All inputs are finite; a program needn't handle non-finite values. No bound on the sum of `events` on one device may be relied on, other than what follows from the above.
Results may differ from a plain program's by a relative error of at most 0.00067.
Values sent between devices are 32-bit elements; how exact they have to be, the bound alone decides.
No kernel may reach another device: no remote copies, remote signals or barrier semaphores. Data moves between devices by JAX's collectives and lax.ppermute only.
A program may use at most 64 MiB of HBM per device.

v0:
```python
import math
import jax
import jax.numpy as jnp
from jax import lax
from jax.sharding import PartitionSpec as P

STRATA = 512
CENTERS_DEV = 16


def prefix(value, axis, join, neutral, backward):
    count, mine = (lax.axis_size(axis), lax.axis_index(axis))
    pieces = jax.tree.map(lambda part: lax.all_gather(part, axis), value)
    if backward:
        pieces = jax.tree.map(lambda part: part[::-1], pieces)
        mine = count - 1 - mine
    so_far = jax.tree.map(
        lambda part, zero: jnp.full_like(part, 0) + jnp.asarray(zero, part.dtype), value, neutral
    )

    def lap(position, so_far):
        longer = join(so_far, jax.tree.map(lambda part: part[position], pieces))
        return jax.tree.map(lambda new, old: jnp.where(position < mine, new, old), longer, so_far)

    return lax.fori_loop(0, count - 1, lap, so_far)


def add_pairs(earlier, later):
    return (earlier[0] + later[0], earlier[1] + later[1])


def add_single(earlier, later):
    return earlier + later


def block_suffix(group_ids, weights, weighted, groups):
    record_count = group_ids.shape[0]
    block_size = min(512, record_count)
    blocks = record_count // block_size
    positions = jnp.arange(block_size)
    upper = positions[None, :] >= positions[:, None]
    labels = jnp.arange(groups)
    contract = (((0,), (0,)), ((), ()))

    def advance(carry, item):
        carry_zero, carry_one = carry
        block_ids, block_weights, block_rows = item
        shared = (block_ids[:, None] == block_ids[None, :]) & upper
        local_one = jnp.dot(
            shared.astype(jnp.bfloat16), block_rows, preferred_element_type=jnp.float32
        )
        local_zero = jnp.dot(
            shared.astype(jnp.float32), block_weights, precision=lax.Precision.HIGHEST
        )
        result = (local_zero + carry_zero[block_ids], local_one + carry_one[block_ids])
        member = block_ids[:, None] == labels[None, :]
        carry_one = carry_one + lax.dot_general(
            member.astype(jnp.bfloat16), block_rows, contract, preferred_element_type=jnp.float32
        )
        carry_zero = carry_zero + jnp.dot(
            block_weights, member.astype(jnp.float32), precision=lax.Precision.HIGHEST
        )
        return ((carry_zero, carry_one), result)

    init = (jnp.zeros((groups,), jnp.float32), jnp.zeros((groups, weighted.shape[1]), jnp.float32))
    items = (
        group_ids.reshape(blocks, block_size),
        weights.reshape(blocks, block_size),
        weighted.reshape(blocks, block_size, weighted.shape[1]),
    )
    totals, outputs = lax.scan(advance, init, items, reverse=True)
    return (
        outputs[0].reshape(record_count),
        outputs[1].reshape(record_count, weighted.shape[1]),
        totals,
    )


def block_prefix(group_ids, increments, groups):
    record_count = group_ids.shape[0]
    block_size = min(512, record_count)
    blocks = record_count // block_size
    positions = jnp.arange(block_size)
    lower = positions[None, :] <= positions[:, None]
    labels = jnp.arange(groups)

    def advance(carry, item):
        block_ids, block_incr = item
        shared = ((block_ids[:, None] == block_ids[None, :]) & lower).astype(jnp.float32)
        result = jnp.dot(shared, block_incr, precision=lax.Precision.HIGHEST) + carry[block_ids]
        member = (block_ids[:, None] == labels[None, :]).astype(jnp.float32)
        return (carry + jnp.dot(block_incr, member, precision=lax.Precision.HIGHEST), result)

    totals, outputs = lax.scan(
        advance,
        jnp.zeros((groups,), jnp.float32),
        (group_ids.reshape(blocks, block_size), increments.reshape(blocks, block_size)),
    )
    return (outputs.reshape(record_count), totals)


def later_moments(totals):
    empty = (jnp.zeros_like(totals[0]), jnp.zeros_like(totals[1]))
    shard_zero, shard_one = lax.psum((totals[0], totals[1]), "rows")
    outer = prefix((shard_zero, shard_one), "tm", add_pairs, empty, True)
    inner = prefix((totals[0], totals[1]), "rows", add_pairs, empty, True)
    return add_pairs(outer, inner)


def earlier_hazard(totals):
    empty = jnp.zeros_like(totals)
    shard_sum = lax.psum(totals, "rows")
    outer = prefix(shard_sum, "tm", add_single, empty, False)
    inner = prefix(totals, "rows", add_single, empty, False)
    return outer + inner


def body(covars, strata, centers, events, counts, beta, frailty):
    record_count = covars.shape[0]
    width = covars.shape[1]
    contract = (((0,), (0,)), ((), ()))
    live = jnp.arange(record_count) < counts[0]
    eta = (
        jnp.dot(covars, beta, precision=lax.Precision.HIGHEST, preferred_element_type=jnp.float32)
        + frailty[centers]
    )
    weights = jnp.where(live, jnp.exp(eta), 0.0)
    weighted = (weights[:, None] * covars.astype(jnp.float32)).astype(jnp.bfloat16)
    suffix_zero, suffix_one, totals = block_suffix(strata, weights, weighted, STRATA)
    later_zero, later_one = later_moments(totals)
    suffix_zero = suffix_zero + later_zero[strata]
    suffix_one = suffix_one + later_one[strata]
    flags = jnp.where(live, events, 0).astype(jnp.float32)
    safe_zero = jnp.where(flags > 0, suffix_zero, 1.0)
    increments = jnp.where(flags > 0, flags / safe_zero, 0.0)
    local_hazard, hazard_totals = block_prefix(strata, increments, STRATA)
    hazard = local_hazard + earlier_hazard(hazard_totals)[strata]
    exposure = weights * hazard
    mean_rows = jnp.where(flags[:, None] > 0, suffix_one / safe_zero[:, None], 0.0)
    mean_low = mean_rows.astype(jnp.bfloat16)
    loaded = (exposure[:, None] * covars.astype(jnp.float32)).astype(jnp.bfloat16)
    gradient = jnp.dot(
        flags.astype(jnp.bfloat16), covars, preferred_element_type=jnp.float32
    ) - jnp.sum(mean_rows, axis=0)
    curvature = lax.dot_general(
        covars, loaded, contract, preferred_element_type=jnp.float32
    ) - lax.dot_general(mean_low, mean_low, contract, preferred_element_type=jnp.float32)
    gradient, curvature = lax.psum((gradient, curvature), ("tm", "rows"))
    devices = lax.axis_size("tm") * lax.axis_size("rows")
    total = record_count * devices
    score = gradient / math.sqrt(total)
    info = curvature / total
    center_total = CENTERS_DEV * devices
    pair = jnp.stack(
        [
            jax.ops.segment_sum(flags - exposure, centers, num_segments=center_total),
            jax.ops.segment_sum(exposure, centers, num_segments=center_total),
        ]
    )
    block_size = min(2048, record_count)
    blocks = record_count // block_size
    labels = jnp.arange(center_total)

    def collect(accum, item):
        block_ids, block_rows = item
        member = (block_ids[:, None] == labels[None, :]).astype(jnp.bfloat16)
        return (
            accum
            + lax.dot_general(member, block_rows, contract, preferred_element_type=jnp.float32),
            None,
        )

    cross, unused_out = lax.scan(
        collect,
        jnp.zeros((center_total, width), jnp.float32),
        (centers.reshape(blocks, block_size), loaded.reshape(blocks, block_size, width)),
    )
    cross_mine, pair_mine = (
        lax.psum_scatter(cross, ("tm", "rows"), scatter_dimension=0, tiled=True),
        lax.psum_scatter(pair, ("tm", "rows"), scatter_dimension=1, tiled=True),
    )
    load = record_count // CENTERS_DEV
    root = math.sqrt(load)
    frailty_mine = lax.dynamic_slice_in_dim(
        frailty, lax.axis_index(("tm", "rows")) * CENTERS_DEV, CENTERS_DEV
    )
    center_score = pair_mine[0] / root - 0.5 * frailty_mine
    center_info = pair_mine[1] / load + 0.5
    center_cross = cross_mine / root
    return (score, info, center_score, center_info, center_cross)


def solution(mesh):
    in_specs = (
        P(("tm", "rows"), None),
        P(("tm", "rows")),
        P(("tm", "rows")),
        P(("tm", "rows")),
        P(("tm", "rows")),
        P(),
        P(),
    )
    out_specs = (P(), P(), P(("tm", "rows")), P(("tm", "rows")), P(("tm", "rows"), None))
    return jax.shard_map(body, mesh=mesh, in_specs=in_specs, out_specs=out_specs, check_vma=False)
```

profile of v0, /device:TPU:0, one launch (start us, length us, event | category | flops | bytes accessed | tf_op | source)
XLA Modules:
  0.0 1883.2 jit_solution(13553118793809692957)
XLA Ops:
  8.6 23.0 %gather_fusion.3 = f32[4096]{0:T(1024)S(1)} fusion(f32[2048]{0:T(1024)S(1)} %copy-done.1, s32[4096]{0:T(1024)S(1)} %fusion.55), kind=kCustom, calls=%fused_computation.3 | custom fusion | bytes 49152 | tf_op jit(solution)/shard_map/gather | solution.py:125
  33.4 1.5 broadcast_in_dim.87
  34.9 58.8 %while.105 = (s32[]{:T(128)}, f32[512]{0:T(512)S(1)}, f32[512,128]{1,0:T(8,128)S(1)}, f32[8,512]{1,0:T(8,128)S(1)}, f32[8,512,128]{2,1,0:T(8,128)}, /*index=5*/f...) while((s32[]{:T(128)}, f32[512]{0:T(512)S(1)}, ...), condition=%wide.region_1.2_spmd.clone, body=%wide.region_0.1_spmd.clone.sunk | while | flops 142807040 | bytes 2419864 | solution.py:71
  35.4 3.5 gather_fusion
  40.6 1.1 fusion.99
  42.8 3.5 gather_fusion
  46.9 1.0 gather_fusion.1
  48.0 1.1 fusion.99
  50.1 3.5 gather_fusion
  55.3 1.1 fusion.99
  57.5 3.5 gather_fusion
  62.7 1.1 fusion.99
  64.9 3.5 gather_fusion
  69.0 1.0 gather_fusion.1
  70.0 1.1 fusion.99
  72.2 3.5 gather_fusion
  76.3 1.0 gather_fusion.1
  77.4 1.0 fusion.99
  79.5 3.5 gather_fusion
  83.7 1.0 gather_fusion.1
  84.7 1.1 fusion.99
  86.9 3.5 gather_fusion
  91.0 1.0 gather_fusion.1
  92.1 1.1 fusion.99
  94.5 26.7 %all-gather.12.cloned.1.call-done = f32[2048,128]{1,0:T(8,128)} async-done(((f32[512,128]{1,0:T(8,128)}), f32[2048,128]{1,0:T(8,128)}) %all-gather.12.cloned.1.call-update) | async-done | bytes 1048592 | tf_op jit(solution)/shard_map/all_gather | solution.py:13
  122.0 44.5 %all-reduce.3.cloned.1.call-done = f32[1,512,128]{2,1,0:T(8,128)} async-done(((f32[1,512,128]{2,1,0:T(8,128)}), f32[1,512,128]{2,1,0:T(8,128)}) %all-reduce.3.cloned.1.call-update) | async-done | bytes 262160 | tf_op jit(solution)/shard_map/psum | solution.py:104
  166.6 9.3 psum.35
  176.0 24.5 %all-gather.3 = f32[32,1,512]{2,1,0:T(1,128)S(1)} all-gather(f32[1,1,512]{2,1,0:T(1,128)S(1)} %bitcast.202), channel_id=1, replica_groups=mesh['tm'=32,'rows'=4] {'tm'}, dimensions={0}, use_global_device_ids=true | all-gather | bytes 67584 | tf_op jit(solution)/shard_map/all_gather | solution.py:13
  200.5 10.4 all-gather.4
  211.1 1.4 rev.15
  212.9 9.2 all-gather.10.cloned.1.call-done
  222.1 7.5 rev.13
  229.7 33.7 %while.106 = (s32[]{:T(128)}, f32[512]{0:T(512)S(1)}, f32[512,128]{1,0:T(8,128)S(1)}, s32[]{:T(128)}, f32[32,512]{1,0:T(8,128)S(1)}, /*index=5*/f32[32,512,128]{2,1,0:T(8,128)}, s32[]{:T(128)}, s32[]{:T(128)}) while((s32[]{:T(128)}, f32[512]{0:T(512)S(1)}, f32[512,128]{1,0:T(8,128)S(1)}, s32[]{:T(128)}, f32[32,512]{1,0:T(8,128)S(1)}, ...), condition=%wide.region_5.6_spmd.clone, body=%wide.region_4.5_spmd.clone.sunk | while | flops 198148 | bytes 796787 | solution.py:25
  263.4 25.9 %gather_fusion.5 = f32[4096]{0:T(1024)S(1)} fusion(f32[512]{0:T(512)S(1)} %add.293, s32[4096]{0:T(1024)S(1)} %fusion.56), kind=kCustom, calls=%fused_computation.5 | custom fusion | bytes 49152 | tf_op jit(solution)/shard_map/gather | solution.py:131
  289.4 37.0 %while.108 = (s32[]{:T(128)}, f32[512]{0:T(512)S(1)}, f32[8,512]{1,0:T(8,128)S(1)}, f32[8,512]{1,0:T(8,128)S(1)}, s32[8,512]{1,0:T(8,128)S(1)}, /*index=5*/s32[]{:T(128)}, s32[]{:T(128)}) while((s32[]{:T(128)}, f32[512]{0:T(512)S(1)}, f32[8,512]{1,0:T(8,128)S(1)}, f32[8,512]{1,0:T(8,128)S(1)}, s32[8,512]{1,0:T(8,128)S(1)}, ...), condition=%wide.region_11.12_spmd.clone, body=%wide.region_10.11_spmd.clone.sunk | while | flops 7344131 | bytes 51303 | solution.py:94
  290.0 3.5 gather_fusion.2
  294.6 3.5 gather_fusion.2
  299.2 3.5 gather_fusion.2
  303.9 3.5 gather_fusion.2
  308.5 3.5 gather_fusion.2
  313.1 3.5 gather_fusion.2
  317.8 3.5 gather_fusion.2
  322.4 3.5 gather_fusion.2
  326.5 10.4 psum.38
  336.9 23.9 %all-gather.5 = f32[32,1,512]{2,1,0:T(1,128)S(1)} all-gather(f32[1,1,512]{2,1,0:T(1,128)S(1)} %bitcast.203), channel_id=1, replica_groups=mesh['tm'=32,'rows'=4] {'tm'}, dimensions={0}, use_global_device_ids=true | all-gather | bytes 67584 | tf_op jit(solution)/shard_map/all_gather | solution.py:13
  360.8 1.7 while.109
  362.5 10.4 all-gather.6
  373.1 25.9 %gather_fusion.6 = f32[4096]{0:T(1024)S(1)} fusion(f32[512]{0:T(512)S(1)} %add.295, s32[4096]{0:T(1024)S(1)} %fusion.56), kind=kCustom, calls=%fused_computation.6 | custom fusion | bytes 49152 | tf_op jit(solution)/shard_map/gather | solution.py:137
  399.1 1.5 fusion.51
  400.6 1.1 convolution_bitcast_fusion.1
  401.7 22.1 %scatter_custom_fusion.1 = f32[2048]{0:T(1024)S(1)} fusion(s32[4096]{0:T(1024)S(1)} %copy-done.7, f32[4096]{0:T(1024)S(1)} %get-tuple-element.902, f32[]{:T(128)} %constant.197.clone.1), kind=kCustom, calls=%fused_computation.112 | custom fusion | flops 4096 | bytes 8196 | tf_op jit(solution)/shard_map/scatter-add | solution.py:157
  423.8 14.2 gather_fusion.4
  438.0 7.1 fusion.52
  445.4 22.1 %scatter_custom_fusion = f32[2048]{0:T(1024)S(1)} fusion(s32[4096]{0:T(1024)S(1)} %copy-done.7, f32[4096]{0:T(1024)S(1)} %get-tuple-element.901, f32[]{:T(128)} %constant.197.clone.1), kind=kCustom, calls=%fused_computation.114 | custom fusion | flops 4096 | bytes 8196 | tf_op jit(solution)/shard_map/scatter-add | solution.py:156
  467.5 1.4 copy.24
  468.9 14.2 while.111
  469.0 7.0 fusion.107
  476.0 7.2 fusion.107
  483.2 3.2 fusion.65
  486.7 62.7 %psum.37 = f32[128]{0:T(128)S(1)} all-reduce(f32[128]{0:T(128)S(1)} %fusion.53), channel_id=1, replica_groups=mesh['tm'=32,'rows'=4] {'tm','rows'}, use_global_device_ids=true, to_apply=%region_9.10 | all-reduce | flops 128 | bytes 1024 | tf_op jit(solution)/shard_map/psum | solution.py:148
  549.9 30.7 %all-reduce.5.cloned.1.call-done = f32[128,128]{0,1:T(8,128)} async-done(((f32[128,128]{0,1:T(8,128)}), f32[128,128]{0,1:T(8,128)}) %all-reduce.5.cloned.1.call-update) | async-done | bytes 65552 | tf_op jit(solution)/shard_map/psum | solution.py:148
  582.2 648.3 %reduce-scatter.7.cloned.1.call-done = f32[16,2]{1,0:T(8,128)} async-done(((f32[2048,2]{1,0:T(8,128)}), f32[16,2]{1,0:T(8,128)}) %reduce-scatter.7.cloned.1.call-update) | async-done | bytes 144
  1232.6 642.5 %reduce-scatter.5.cloned.1.call-done = f32[16,128]{1,0:T(8,128)} async-done(((f32[2048,128]{1,0:T(8,128)}), f32[16,128]{1,0:T(8,128)}) %reduce-scatter.5.cloned.1.call-update) | async-done | bytes 8208 | tf_op jit(solution)/shard_map/reduce_scatter | solution.py:179
  1875.1 1.3 broadcast_multiply_fusion.1
  (380 shorter events, 68.7 us)
Async XLA Ops:
  7.2 24.5 %copy-start = (f32[128]{0:T(128)S(1)}, f32[128]{0:T(128)}, u32[]{:S(2)}) copy-start(f32[128]{0:T(128)} %param.26) | copy-start | bytes 1540
  7.2 1.4 copy-start.1
  7.2 114.0 %all-gather.12.cloned.1.call-start = ((), (), s32[]{:S(2)}) async-start(), calls=%async_computation.6 | async-start | bytes 1310720 | tf_op jit(solution)/shard_map/all_gather | solution.py:13
  8.6 23.1 %copy-start.2 = (bf16[4096,128]{1,0:T(8,128)(2,1)S(1)}, bf16[4096,128]{1,0:T(8,128)(2,1)}, u32[]{:S(2)}) copy-start(bf16[4096,128]{1,0:T(8,128)(2,1)} %param.21) | copy-start | bytes 3145732
  31.7 1.7 copy-start.6
  34.9 131.7 %copy-start.7 = (s32[4096]{0:T(1024)S(1)}, s32[4096]{0:T(1024)}, u32[]{:S(2)}) copy-start(s32[4096]{0:T(1024)} %param.23) | copy-start | bytes 49156
  93.7 0.7 copy-start.3
  121.2 45.3 %all-reduce.3.cloned.1.call-start = ((), (), s32[]{:S(2)}) async-start(), calls=%async_computation.2 | async-start | bytes 524288 | tf_op jit(solution)/shard_map/psum | solution.py:104
  121.9 100.2 %all-gather.10.cloned.1.call-start = ((), (), s32[]{:S(2)}) async-start(), calls=%async_computation.3 | async-start | bytes 8650752 | tf_op jit(solution)/shard_map/all_gather | solution.py:13
  166.5 414.2 %all-reduce.5.cloned.1.call-start = ((), (), s32[]{:S(2)}) async-start(), calls=%async_computation.4 | async-start | bytes 131072 | tf_op jit(solution)/shard_map/psum | solution.py:148
  263.4 26.0 %copy-start.5 = (s32[4096]{0:T(1024)S(1)}, s32[4096]{0:T(1024)}, u32[]{:S(2)}) copy-start(s32[4096]{0:T(1024)} %param.24) | copy-start | bytes 49156
  445.2 785.3 %reduce-scatter.7.cloned.1.call-start = ((), (), s32[]{:S(2)}) async-start(), calls=%async_computation.7 | async-start | bytes 1056768
  468.9 1406.2 %reduce-scatter.5.cloned.1.call-start = ((), (), s32[]{:S(2)}) async-start(), calls=%async_computation.5 | async-start | bytes 1056768 | tf_op jit(solution)/shard_map/reduce_scatter | solution.py:179
  468.9 14.3 copy-start.4
Sparse Core Ops, SparseCore 0:
  94.6 26.5 all-gather.11
  124.3 42.1 all-reduce.2
  168.7 53.3 all-gather.9
  445.3 135.3 all-reduce.4
  582.8 647.6 reduce-scatter.6
  1232.7 642.3 reduce-scatter.4
where the time goes:
time: 1880 us
  waiting for transfers between devices  1400 us (74%)
  local copies, waits for them, and re-layouts  170 us (9%)
  blocking collectives  152 us (8%)
  other arithmetic  88.2 us (5%)
  matrix products  52 us (3%)
    unnamed x7, waiting for transfers between devices  649 us
    reduce_scatter x1, waiting for transfers between devices, body(): lax.psum_scatter(cross, ('tm', 'rows'), scatter_dimension=0, tiled=True)  642 us
    all_gather x4, blocking collectives, prefix(): pieces = jax.tree.map(lambda part: lax.all_gather(part, axis), value)  69.2 us
    psum x1, blocking collectives, body(): gradient, curvature = lax.psum((gradient, curvature), ('tm', 'rows'))  62.7 us
    psum x1, waiting for transfers between devices, later_moments(): shard_zero, shard_one = lax.psum((totals[0], totals[1]), 'rows')  44.5 us
  transfers between devices with their start and end apart: 6, of which 6 were waited for; matrix products, arithmetic and copies ran while one was open for 3% of the time, Pallas kernels for 0%

commit v1 on v0

--- a/solution.py
+++ b/solution.py
@@ -6,6 +6,12 @@
 
 STRATA = 512
 CENTERS_DEV = 16
+
+
+def _edit_sectors(panel):
+    item_now = lax.psum(panel, "tm")
+    block_now = lax.psum(item_now, "rows")
+    return block_now
 
 
 def prefix(value, axis, join, neutral, backward):
@@ -145,7 +151,7 @@
     curvature = lax.dot_general(
         covars, loaded, contract, preferred_element_type=jnp.float32
     ) - lax.dot_general(mean_low, mean_low, contract, preferred_element_type=jnp.float32)
-    gradient, curvature = lax.psum((gradient, curvature), ("tm", "rows"))
+    gradient, curvature = _edit_sectors((gradient, curvature))
     devices = lax.axis_size("tm") * lax.axis_size("rows")
     total = record_count * devices
     score = gradient / math.sqrt(total)

time: 1880 us -> 1950 us (1.037)
  waiting for transfers between devices: 1400 us -> 1470 us
    psum x1 -> x2, waiting for transfers between devices: 30.7 us -> 107 us  [the longest x1 71.8 us: _edit_sectors(): item_now = lax.psum(panel, 'tm')]
    unnamed x7 -> x8, waiting for transfers between devices: 649 us -> 636 us
  transfers between devices with their start and end apart: 6 -> 7, of which waited for: 6 -> 7; matrix products, arithmetic and copies ran while one was open for 3% -> 2% of each run, Pallas kernels for 0% -> 0%
where the time goes in v1:
time: 1950 us
  waiting for transfers between devices  1470 us (75%)
  local copies, waits for them, and re-layouts  171 us (9%)
  blocking collectives  152 us (8%)
  other arithmetic  87.9 us (5%)
  matrix products  47.2 us (2%)
    reduce_scatter x1, waiting for transfers between devices, body(): lax.psum_scatter(cross, ('tm', 'rows'), scatter_dimension=0, tiled=True)  648 us
    unnamed x8, waiting for transfers between devices  636 us
    psum x1, waiting for transfers between devices, _edit_sectors(): item_now = lax.psum(panel, 'tm')  71.8 us
    all_gather x4, blocking collectives, prefix(): pieces = jax.tree.map(lambda part: lax.all_gather(part, axis), value)  66.6 us
    psum x1, blocking collectives, _edit_sectors(): item_now = lax.psum(panel, 'tm')  65.5 us
    psum x1, waiting for transfers between devices, later_moments(): shard_zero, shard_one = lax.psum((totals[0], totals[1]), 'rows')  44.5 us
  transfers between devices with their start and end apart: 7, of which 7 were waited for; matrix products, arithmetic and copies ran while one was open for 2% of the time, Pallas kernels for 0%

profile of v1, /device:TPU:0, one launch (start us, length us, event | category | flops | bytes accessed | tf_op | source)
XLA Modules:
  0.0 1948.0 jit_solution(4758874101425940531)
XLA Ops:
  8.6 23.0 %gather_fusion.3 = f32[4096]{0:T(1024)S(1)} fusion(f32[2048]{0:T(1024)S(1)} %copy-done.1, s32[4096]{0:T(1024)S(1)} %fusion.55), kind=kCustom, calls=%fused_computation.3 | custom fusion | bytes 49152 | tf_op jit(solution)/shard_map/gather | solution.py:131
  33.4 1.5 broadcast_in_dim.87
  34.9 58.8 %while.105 = (s32[]{:T(128)}, f32[512]{0:T(512)S(1)}, f32[512,128]{1,0:T(8,128)S(1)}, f32[8,512]{1,0:T(8,128)S(1)}, f32[8,512,128]{2,1,0:T(8,128)}, /*index=5*/f...) while((s32[]{:T(128)}, f32[512]{0:T(512)S(1)}, ...), condition=%wide.region_1.2_spmd.clone, body=%wide.region_0.1_spmd.clone.sunk | while | flops 142807040 | bytes 2419864 | solution.py:77
  35.4 3.5 gather_fusion
  40.6 1.1 fusion.99
  42.8 3.5 gather_fusion
  46.9 1.0 gather_fusion.1
  48.0 1.1 fusion.99
  50.1 3.5 gather_fusion
  55.3 1.1 fusion.99
  57.5 3.5 gather_fusion
  62.7 1.1 fusion.99
  64.9 3.5 gather_fusion
  69.0 1.0 gather_fusion.1
  70.0 1.1 fusion.99
  72.2 3.5 gather_fusion
  76.4 1.0 gather_fusion.1
  77.4 1.1 fusion.99
  79.6 3.5 gather_fusion
  83.7 1.0 gather_fusion.1
  84.7 1.1 fusion.99
  86.9 3.5 gather_fusion
  91.1 1.0 gather_fusion.1
  92.1 1.0 fusion.99
  94.4 26.7 %all-gather.12.cloned.1.call-done = f32[2048,128]{1,0:T(8,128)} async-done(((f32[512,128]{1,0:T(8,128)}), f32[2048,128]{1,0:T(8,128)}) %all-gather.12.cloned.1.call-update) | async-done | bytes 1048592 | tf_op jit(solution)/shard_map/all_gather | solution.py:19
  121.9 44.5 %all-reduce.5.cloned.1.call-done = f32[1,512,128]{2,1,0:T(8,128)} async-done(((f32[1,512,128]{2,1,0:T(8,128)}), f32[1,512,128]{2,1,0:T(8,128)}) %all-reduce.5.cloned.1.call-update) | async-done | bytes 262160 | tf_op jit(solution)/shard_map/psum | solution.py:110
  166.6 9.3 psum.49
  175.9 24.5 %all-gather.3 = f32[32,1,512]{2,1,0:T(1,128)S(1)} all-gather(f32[1,1,512]{2,1,0:T(1,128)S(1)} %bitcast.202), channel_id=1, replica_groups=mesh['tm'=32,'rows'=4] {'tm'}, dimensions={0}, use_global_device_ids=true | all-gather | bytes 67584 | tf_op jit(solution)/shard_map/all_gather | solution.py:19
  200.5 10.4 all-gather.4
  211.1 1.4 rev.15
  212.9 9.2 all-gather.10.cloned.1.call-done
  222.1 7.5 rev.13
  229.6 33.7 %while.106 = (s32[]{:T(128)}, f32[512]{0:T(512)S(1)}, f32[512,128]{1,0:T(8,128)S(1)}, s32[]{:T(128)}, f32[32,512]{1,0:T(8,128)S(1)}, /*index=5*/f32[32,512,128]{2,1,0:T(8,128)}, s32[]{:T(128)}, s32[]{:T(128)}) while((s32[]{:T(128)}, f32[512]{0:T(512)S(1)}, f32[512,128]{1,0:T(8,128)S(1)}, s32[]{:T(128)}, f32[32,512]{1,0:T(8,128)S(1)}, ...), condition=%wide.region_5.6_spmd.clone, body=%wide.region_4.5_spmd.clone.sunk | while | flops 198148 | bytes 796787 | solution.py:31
  263.4 25.9 %gather_fusion.5 = f32[4096]{0:T(1024)S(1)} fusion(f32[512]{0:T(512)S(1)} %add.297, s32[4096]{0:T(1024)S(1)} %fusion.56), kind=kCustom, calls=%fused_computation.5 | custom fusion | bytes 49152 | tf_op jit(solution)/shard_map/gather | solution.py:137
  289.4 14.1 gather_fusion.4
  303.5 3.5 fusion.65
  307.3 65.5 %psum.51 = f32[128]{0:T(128)S(1)} all-reduce(f32[128]{0:T(128)S(1)} %fusion.53), channel_id=1, replica_groups=mesh['tm'=32,'rows'=4] {'tm'}, use_global_device_ids=true, to_apply=%region_9.10 | all-reduce | flops 128 | bytes 1024 | tf_op jit(solution)/shard_map/psum | solution.py:12
  372.8 37.0 %while.108 = (s32[]{:T(128)}, f32[512]{0:T(512)S(1)}, f32[8,512]{1,0:T(8,128)S(1)}, f32[8,512]{1,0:T(8,128)S(1)}, s32[8,512]{1,0:T(8,128)S(1)}, /*index=5*/s32[]{:T(128)}, s32[]{:T(128)}) while((s32[]{:T(128)}, f32[512]{0:T(512)S(1)}, f32[8,512]{1,0:T(8,128)S(1)}, f32[8,512]{1,0:T(8,128)S(1)}, s32[8,512]{1,0:T(8,128)S(1)}, ...), condition=%wide.region_12.13_spmd.clone, body=%wide.region_11.12_spmd.clone.sunk | while | flops 7344131 | bytes 51303 | solution.py:100
  373.3 3.5 gather_fusion.2
  378.0 3.5 gather_fusion.2
  382.6 3.5 gather_fusion.2
  387.2 3.5 gather_fusion.2
  391.9 3.5 gather_fusion.2
  396.5 3.5 gather_fusion.2
  401.1 3.5 gather_fusion.2
  405.7 3.5 gather_fusion.2
  409.8 10.4 all-reduce
  420.3 21.2 %all-gather.5 = f32[32,1,512]{2,1,0:T(1,128)S(1)} all-gather(f32[1,1,512]{2,1,0:T(1,128)S(1)} %bitcast.203), channel_id=1, replica_groups=mesh['tm'=32,'rows'=4] {'tm'}, dimensions={0}, use_global_device_ids=true | all-gather | bytes 67584 | tf_op jit(solution)/shard_map/all_gather | solution.py:19
  441.5 1.7 while.109
  443.2 10.4 all-gather.6
  453.8 25.9 %gather_fusion.6 = f32[4096]{0:T(1024)S(1)} fusion(f32[512]{0:T(512)S(1)} %add.299, s32[4096]{0:T(1024)S(1)} %fusion.56), kind=kCustom, calls=%fused_computation.6 | custom fusion | bytes 49152 | tf_op jit(solution)/shard_map/gather | solution.py:143
  479.8 1.1 convolution_bitcast_fusion.1
  480.9 22.2 %scatter_custom_fusion.1 = f32[2048]{0:T(1024)S(1)} fusion(s32[4096]{0:T(1024)S(1)} %copy-done.9, f32[4096]{0:T(1024)S(1)} %get-tuple-element.904, f32[]{:T(128)} %constant.197.clone.1), kind=kCustom, calls=%fused_computation.112 | custom fusion | flops 4096 | bytes 8196 | tf_op jit(solution)/shard_map/scatter-add | solution.py:163
  503.2 6.0 fusion.52
  509.3 22.1 %scatter_custom_fusion = f32[2048]{0:T(1024)S(1)} fusion(s32[4096]{0:T(1024)S(1)} %copy-done.9, f32[4096]{0:T(1024)S(1)} %get-tuple-element.903, f32[]{:T(128)} %constant.197.clone.1), kind=kCustom, calls=%fused_computation.114 | custom fusion | flops 4096 | bytes 8196 | tf_op jit(solution)/shard_map/scatter-add | solution.py:162
  531.4 1.4 copy.24
  533.5 71.8 %all-reduce.7.cloned.1.call-done = f32[128,128]{0,1:T(8,128)} async-done(((f32[128,128]{0,1:T(8,128)}), f32[128,128]{0,1:T(8,128)}) %all-reduce.7.cloned.1.call-update) | async-done | bytes 65552 | tf_op jit(solution)/shard_map/psum | solution.py:12
  605.4 10.5 while.111
  605.4 5.2 fusion.107
  610.7 5.2 fusion.107
  617.5 635.7 %reduce-scatter.7.cloned.1.call-done = f32[16,2]{1,0:T(8,128)} async-done(((f32[2048,2]{1,0:T(8,128)}), f32[16,2]{1,0:T(8,128)}) %reduce-scatter.7.cloned.1.call-update) | async-done | bytes 144
  1255.3 35.4 %all-reduce.9.cloned.1.call-done = f32[128,128]{0,1:T(8,128)} async-done(((f32[128,128]{0,1:T(8,128)}), f32[128,128]{0,1:T(8,128)}) %all-reduce.9.cloned.1.call-update) | async-done | bytes 65552 | tf_op jit(solution)/shard_map/psum | solution.py:13
  1292.2 647.6 %reduce-scatter.5.cloned.1.call-done = f32[16,128]{1,0:T(8,128)} async-done(((f32[2048,128]{1,0:T(8,128)}), f32[16,128]{1,0:T(8,128)}) %reduce-scatter.5.cloned.1.call-update) | async-done | bytes 8208 | tf_op jit(solution)/shard_map/reduce_scatter | solution.py:185
  1939.8 1.3 broadcast_multiply_fusion.1
  (387 shorter events, 70.3 us)
Async XLA Ops:
  7.2 24.5 %copy-start = (f32[128]{0:T(128)S(1)}, f32[128]{0:T(128)}, u32[]{:S(2)}) copy-start(f32[128]{0:T(128)} %param.26) | copy-start | bytes 1540
  7.2 1.4 copy-start.1
  7.2 114.0 %all-gather.12.cloned.1.call-start = ((), (), s32[]{:S(2)}) async-start(), calls=%async_computation.7 | async-start | bytes 1310720 | tf_op jit(solution)/shard_map/all_gather | solution.py:19
  8.6 23.1 %copy-start.2 = (bf16[4096,128]{1,0:T(8,128)(2,1)S(1)}, bf16[4096,128]{1,0:T(8,128)(2,1)}, u32[]{:S(2)}) copy-start(bf16[4096,128]{1,0:T(8,128)(2,1)} %param.21) | copy-start | bytes 3145732
  31.7 1.7 copy-start.8
  34.9 131.7 %copy-start.9 = (s32[4096]{0:T(1024)S(1)}, s32[4096]{0:T(1024)}, u32[]{:S(2)}) copy-start(s32[4096]{0:T(1024)} %param.23) | copy-start | bytes 49156
  34.9 176.2 %copy-start.7 = (s32[4096]{0:T(1024)S(1)}, s32[4096]{0:T(1024)}, u32[]{:S(2)}) copy-start(s32[4096]{0:T(1024)} %param.24) | copy-start | bytes 49156
  93.7 0.7 copy-start.3
  121.2 45.3 %all-reduce.5.cloned.1.call-start = ((), (), s32[]{:S(2)}) async-start(), calls=%async_computation.2 | async-start | bytes 524288 | tf_op jit(solution)/shard_map/psum | solution.py:110
  121.9 100.2 %all-gather.10.cloned.1.call-start = ((), (), s32[]{:S(2)}) async-start(), calls=%async_computation.3 | async-start | bytes 8650752 | tf_op jit(solution)/shard_map/all_gather | solution.py:19
  166.5 438.9 %all-reduce.7.cloned.1.call-start = ((), (), s32[]{:S(2)}) async-start(), calls=%async_computation.4 | async-start | bytes 131072 | tf_op jit(solution)/shard_map/psum | solution.py:12
  479.8 23.4 %copy-start.4 = (f32[8,512,128]{2,1,0:T(8,128)S(1)}, f32[8,512,128]{2,1,0:T(8,128)}, u32[]{:S(2)}) copy-start(f32[8,512,128]{2,1,0:T(8,128)} %get-tuple-element.649) | copy-start | bytes 6291460
  509.2 743.9 %reduce-scatter.7.cloned.1.call-start = ((), (), s32[]{:S(2)}) async-start(), calls=%async_computation.8 | async-start | bytes 1056768
  531.4 74.0 %copy-start.5 = (f32[2048,128]{1,0:T(8,128)S(1)}, f32[2048,128]{1,0:T(8,128)}, u32[]{:S(2)}) copy-start(f32[2048,128]{1,0:T(8,128)} %custom-call.9) | copy-start | bytes 3145732
  532.7 757.9 %all-reduce.9.cloned.1.call-start = ((), (), s32[]{:S(2)}) async-start(), calls=%async_computation.5 | async-start | bytes 131072 | tf_op jit(solution)/shard_map/psum | solution.py:13
  605.4 1334.5 %reduce-scatter.5.cloned.1.call-start = ((), (), s32[]{:S(2)}) async-start(), calls=%async_computation.6 | async-start | bytes 1056768 | tf_op jit(solution)/shard_map/reduce_scatter | solution.py:185
  616.0 1.0 copy-start.6
Sparse Core Ops, SparseCore 0:
  94.6 26.5 all-gather.11
  124.3 42.1 all-reduce.4
  168.7 53.3 all-gather.9
  509.4 95.9 all-reduce.6
  607.5 645.5 reduce-scatter.6
  1255.3 35.2 all-reduce.8
  1293.0 646.8 reduce-scatter.4
